TPU v7x, 256 devices: a whole 4x4x8 slice. The times are simulated.
256 devices in a mesh: section: 16 (over z, y_lo), tile: 16 (over x, y_hi, core).
Axes of the slice: x: 4, y: 4 (y_hi: 2, y_lo: 2; y = y_hi * 2 + y_lo), z: 8, core: 2. Of those that a mesh axis runs over, the one named last changes fastest.
Arguments:
- acts: bfloat16 [16, 2, 256, 128, 128], P('section', None, None, 'tile'), may hold values from -6 to 6
- weights: bfloat16 [16, 9, 256, 256], P('section'), may hold values from -0.0625 to 0.0625
- cotangent: bfloat16 [2, 256, 128, 128], P(None, None, 'tile'), may hold values from -6 to 6
Outputs:
- grad_acts: bfloat16 [16, 2, 256, 128, 128], P('section', None, None, 'tile')
- weight_grad: float32 [16, 9, 256, 256], P('section')
All inputs are finite; a program needn't handle non-finite values.
Results may differ from a plain program's by a relative error of at most 0.017.
Values may be sent and summed in bfloat16 or wider, within the bound.
No kernel may reach another device: no remote copies, remote signals or barrier semaphores. Data moves between devices by JAX's collectives and lax.ppermute only.
A program may use at most 64 MiB of HBM per device.

v0:
```python
import jax
import jax.numpy as jnp
from jax import lax
from jax.sharding import PartitionSpec as P


def padded_2(block, sides, width):
    for axis, dim in sides:
        count = lax.axis_size(axis)
        forward = [(i, i + 1) for i in range(count - 1)]
        forward.append((count - 1, 0))
        backward = [(target, source) for source, target in forward]
        low = lax.ppermute(
            lax.slice_in_dim(block, block.shape[dim] - width, None, axis=dim), axis, forward
        )
        high = lax.ppermute(lax.slice_in_dim(block, 0, width, axis=dim), axis, backward)
        block = jnp.concatenate([low, block, high], axis=dim)
    return block


def from_behind(block, axis, distance):
    devices = range(lax.axis_size(axis))
    route = [(i - distance, i) for i in devices if i - distance in devices]
    return lax.ppermute(block, axis, route)


def shift_cols(field, offset):
    if offset == 0:
        return field
    zeros = jnp.zeros_like(field[..., :1])
    if offset == 1:
        return jnp.concatenate([field[..., 1:], zeros], axis=-1)
    return jnp.concatenate([zeros, field[..., :-1]], axis=-1)


def back_conv(padded, kernel, height):
    total = jnp.zeros(padded.shape[:2] + (height, padded.shape[3]), jnp.float32)
    for row_step in (-1, 0, 1):
        rows_cut = padded[:, :, 1 - row_step : 1 - row_step + height, :]
        for col_step in (-1, 0, 1):
            index = (row_step + 1) * 3 + col_step + 1
            moved = shift_cols(rows_cut, -col_step)
            total = total + jnp.einsum(
                "oi,gorc->girc", kernel[index], moved, preferred_element_type=jnp.float32
            )
    return total


def kernel_grad(padded, hidden_rims, height):
    grad_mid = padded[:, :, 1 : 1 + height, :]
    parts = []
    for row_step in (-1, 0, 1):
        rows_cut = hidden_rims[:, :, 1 + row_step : 1 + row_step + height, :]
        for col_step in (-1, 0, 1):
            seen = shift_cols(rows_cut, col_step)
            parts.append(
                jnp.einsum("gorc,girc->oi", grad_mid, seen, preferred_element_type=jnp.float32)
            )
    return jnp.stack(parts)


def per_device(acts, weights, cotangent):
    n_section = lax.axis_size("section")
    section_id = lax.axis_index("section")
    inputs = acts[0].astype(jnp.float32)
    kernel = weights[0]
    batches, chans, height, width = acts.shape[1:]
    sigma = jax.nn.sigmoid(inputs)
    hidden = (inputs * sigma).astype(jnp.bfloat16)
    slope = sigma * (1.0 + inputs * (1.0 - sigma))
    hidden_rims = padded_2(hidden, (("tile", 2),), 1)
    scale = 1.0 / jnp.sqrt(jnp.float32(batches * height * lax.axis_size("tile") * width))
    n_groups = batches // batches
    ticks = n_section + n_groups - 1

    def one_tick(carry, tick):
        incoming, grads, kernel_acc, stored = carry
        batch_id = tick - (n_section - 1 - section_id)
        valid = jnp.logical_and(batch_id >= 0, batch_id < n_groups)
        upper = jnp.where(section_id == n_section - 1, cotangent, incoming)
        padded = padded_2(upper, (("tile", 2),), 1)

        def active(operands):
            padded_in, upper_in, slope_in, rims_in = operands
            back = back_conv(padded_in, kernel, height)
            lowered = (upper_in.astype(jnp.float32) + back * slope_in).astype(jnp.bfloat16)
            partial_k = kernel_grad(padded_in, rims_in, height)
            return (lowered, partial_k)

        def resting(operands):
            return (jnp.zeros(upper.shape, jnp.bfloat16), jnp.zeros(kernel_acc.shape, jnp.float32))

        lowered, partial_k = lax.cond(valid, active, resting, (padded, upper, slope, hidden_rims))
        kernel_acc = kernel_acc + partial_k
        old_grads = grads
        grads = jnp.where(valid, lowered, old_grads)
        old_store = stored
        stored = jnp.where(valid, padded, old_store)
        outgoing = from_behind(lowered, "section", -1)
        return ((outgoing, grads, kernel_acc, stored), None)

    initial = (
        jnp.zeros((batches, chans, height, width), jnp.bfloat16),
        jnp.zeros((batches, chans, height, width), jnp.bfloat16),
        jnp.zeros((9, chans, chans), jnp.float32),
        jnp.zeros((batches, chans, height + 2, width), jnp.bfloat16),
    )
    final, unused = lax.scan(one_tick, initial, jnp.arange(ticks, dtype=jnp.int32))
    grads = final[1]
    kernel_acc = final[2]
    weight_grad = lax.psum(kernel_acc * scale, "tile")
    return (grads[None], weight_grad[None])


def solution(mesh):
    placed = (
        P("section", None, None, "tile", None),
        P("section", None, None, None),
        P(None, None, "tile", None),
    )
    return jax.shard_map(
        per_device,
        mesh=mesh,
        in_specs=placed,
        out_specs=(P("section", None, None, "tile", None), P("section", None, None, None)),
        check_vma=False,
    )
```

profile of v0, /device:TPU:1, one launch (start us, length us, event | category | flops | bytes accessed | tf_op | source)
XLA Modules:
  0.0 1089.7 jit_solution(17540240250807122509)
XLA Ops:
  7.2 3.6 fusion.66
  10.8 4.4 collective-permute-start.3
  16.7 2.9 copy.19
  19.5 2.9 collective-permute-done.4
  23.7 900.9 %while.17 = (s32[]{:T(128)}, bf16[2,256,8,128]{1,3,2,0:T(8,128)(2,1)}, bf16[2,256,8,128]{1,3,2,0:T(8,128)(2,1)}, f32[9,256,256]{1,2,0:T(8,128)}, s32[16]{0:T(128...) while((s32[]{:T(128)}, ...), condition=%wide.region_3.4_spmd.clone, body=%wide.region_0.3_spmd.clone.sunk | while | flops 4842192896 | bytes 153502240 | solution.py:108
  41.6 13.8 %collective-permute-done.2 = bf16[2,256,8,128]{1,3,2,0:T(8,128)(2,1)S(1)} collective-permute-done((bf16[2,256,8,128]{1,3,2,0:T(8,128)(2,1)}, bf16[2,256,8,128]{1,3,2,0:T(8,128)(2,1)S(1)}, u32[]{:S(2)}, u32[]{:S(2)}) %collective-permute-start.2) | collective-permute-done | bytes 1048608 | tf_op jit(solution)/shard_map/while/body/eval_jaxpr/ppermute | solution.py:24
  58.4 8.1 collective-permute-start
  82.0 13.3 %collective-permute-done.2 = bf16[2,256,8,128]{1,3,2,0:T(8,128)(2,1)S(1)} collective-permute-done((bf16[2,256,8,128]{1,3,2,0:T(8,128)(2,1)}, bf16[2,256,8,128]{1,3,2,0:T(8,128)(2,1)S(1)}, u32[]{:S(2)}, u32[]{:S(2)}) %collective-permute-start.2) | collective-permute-done | bytes 1048608 | tf_op jit(solution)/shard_map/while/body/eval_jaxpr/ppermute | solution.py:24
  98.4 8.1 collective-permute-start
  113.2 2.7 conditional.3
  122.2 14.2 %collective-permute-done.2 = bf16[2,256,8,128]{1,3,2,0:T(8,128)(2,1)S(1)} collective-permute-done((bf16[2,256,8,128]{1,3,2,0:T(8,128)(2,1)}, bf16[2,256,8,128]{1,3,2,0:T(8,128)(2,1)S(1)}, u32[]{:S(2)}, u32[]{:S(2)}) %collective-permute-start.2) | collective-permute-done | bytes 1048608 | tf_op jit(solution)/shard_map/while/body/eval_jaxpr/ppermute | solution.py:24
  139.4 7.8 collective-permute-start
  154.6 2.7 conditional.3
  163.6 14.5 %collective-permute-done.2 = bf16[2,256,8,128]{1,3,2,0:T(8,128)(2,1)S(1)} collective-permute-done((bf16[2,256,8,128]{1,3,2,0:T(8,128)(2,1)}, bf16[2,256,8,128]{1,3,2,0:T(8,128)(2,1)S(1)}, u32[]{:S(2)}, u32[]{:S(2)}) %collective-permute-start.2) | collective-permute-done | bytes 1048608 | tf_op jit(solution)/shard_map/while/body/eval_jaxpr/ppermute | solution.py:24
  181.1 6.9 collective-permute-start
  188.0 3.7 collective-permute-start.1
  196.4 2.7 conditional.3
  205.3 17.4 %collective-permute-done.2 = bf16[2,256,8,128]{1,3,2,0:T(8,128)(2,1)S(1)} collective-permute-done((bf16[2,256,8,128]{1,3,2,0:T(8,128)(2,1)}, bf16[2,256,8,128]{1,3,2,0:T(8,128)(2,1)S(1)}, u32[]{:S(2)}, u32[]{:S(2)}) %collective-permute-start.2) | collective-permute-done | bytes 1048608 | tf_op jit(solution)/shard_map/while/body/eval_jaxpr/ppermute | solution.py:24
  225.7 4.1 collective-permute-start
  236.3 2.7 conditional.3
  245.3 17.5 %collective-permute-done.2 = bf16[2,256,8,128]{1,3,2,0:T(8,128)(2,1)S(1)} collective-permute-done((bf16[2,256,8,128]{1,3,2,0:T(8,128)(2,1)}, bf16[2,256,8,128]{1,3,2,0:T(8,128)(2,1)S(1)}, u32[]{:S(2)}, u32[]{:S(2)}) %collective-permute-start.2) | collective-permute-done | bytes 1048608 | tf_op jit(solution)/shard_map/while/body/eval_jaxpr/ppermute | solution.py:24
  265.8 4.2 collective-permute-start
  275.6 2.7 conditional.3
  284.6 16.7 %collective-permute-done.2 = bf16[2,256,8,128]{1,3,2,0:T(8,128)(2,1)S(1)} collective-permute-done((bf16[2,256,8,128]{1,3,2,0:T(8,128)(2,1)}, bf16[2,256,8,128]{1,3,2,0:T(8,128)(2,1)S(1)}, u32[]{:S(2)}, u32[]{:S(2)}) %collective-permute-start.2) | collective-permute-done | bytes 1048608 | tf_op jit(solution)/shard_map/while/body/eval_jaxpr/ppermute | solution.py:24
  304.4 5.0 collective-permute-start
  314.9 2.7 conditional.3
  323.9 16.6 %collective-permute-done.2 = bf16[2,256,8,128]{1,3,2,0:T(8,128)(2,1)S(1)} collective-permute-done((bf16[2,256,8,128]{1,3,2,0:T(8,128)(2,1)}, bf16[2,256,8,128]{1,3,2,0:T(8,128)(2,1)S(1)}, u32[]{:S(2)}, u32[]{:S(2)}) %collective-permute-start.2) | collective-permute-done | bytes 1048608 | tf_op jit(solution)/shard_map/while/body/eval_jaxpr/ppermute | solution.py:24
  343.5 5.1 collective-permute-start
  363.0 16.5 %collective-permute-done.2 = bf16[2,256,8,128]{1,3,2,0:T(8,128)(2,1)S(1)} collective-permute-done((bf16[2,256,8,128]{1,3,2,0:T(8,128)(2,1)}, bf16[2,256,8,128]{1,3,2,0:T(8,128)(2,1)S(1)}, u32[]{:S(2)}, u32[]{:S(2)}) %collective-permute-start.2) | collective-permute-done | bytes 1048608 | tf_op jit(solution)/shard_map/while/body/eval_jaxpr/ppermute | solution.py:24
  382.5 5.2 collective-permute-start
  393.0 2.7 conditional.3
  402.0 16.5 %collective-permute-done.2 = bf16[2,256,8,128]{1,3,2,0:T(8,128)(2,1)S(1)} collective-permute-done((bf16[2,256,8,128]{1,3,2,0:T(8,128)(2,1)}, bf16[2,256,8,128]{1,3,2,0:T(8,128)(2,1)S(1)}, u32[]{:S(2)}, u32[]{:S(2)}) %collective-permute-start.2) | collective-permute-done | bytes 1048608 | tf_op jit(solution)/shard_map/while/body/eval_jaxpr/ppermute | solution.py:24
  421.5 5.4 collective-permute-start
  441.1 17.7 %collective-permute-done.2 = bf16[2,256,8,128]{1,3,2,0:T(8,128)(2,1)S(1)} collective-permute-done((bf16[2,256,8,128]{1,3,2,0:T(8,128)(2,1)}, bf16[2,256,8,128]{1,3,2,0:T(8,128)(2,1)S(1)}, u32[]{:S(2)}, u32[]{:S(2)}) %collective-permute-start.2) | collective-permute-done | bytes 1048608 | tf_op jit(solution)/shard_map/while/body/eval_jaxpr/ppermute | solution.py:24
  461.8 5.4 collective-permute-start
  482.0 17.2 %collective-permute-done.2 = bf16[2,256,8,128]{1,3,2,0:T(8,128)(2,1)S(1)} collective-permute-done((bf16[2,256,8,128]{1,3,2,0:T(8,128)(2,1)}, bf16[2,256,8,128]{1,3,2,0:T(8,128)(2,1)S(1)}, u32[]{:S(2)}, u32[]{:S(2)}) %collective-permute-start.2) | collective-permute-done | bytes 1048608 | tf_op jit(solution)/shard_map/while/body/eval_jaxpr/ppermute | solution.py:24
  502.2 5.4 collective-permute-start
  522.5 17.0 %collective-permute-done.2 = bf16[2,256,8,128]{1,3,2,0:T(8,128)(2,1)S(1)} collective-permute-done((bf16[2,256,8,128]{1,3,2,0:T(8,128)(2,1)}, bf16[2,256,8,128]{1,3,2,0:T(8,128)(2,1)S(1)}, u32[]{:S(2)}, u32[]{:S(2)}) %collective-permute-start.2) | collective-permute-done | bytes 1048608 | tf_op jit(solution)/shard_map/while/body/eval_jaxpr/ppermute | solution.py:24
  542.5 5.4 collective-permute-start
  562.8 16.8 %collective-permute-done.2 = bf16[2,256,8,128]{1,3,2,0:T(8,128)(2,1)S(1)} collective-permute-done((bf16[2,256,8,128]{1,3,2,0:T(8,128)(2,1)}, bf16[2,256,8,128]{1,3,2,0:T(8,128)(2,1)S(1)}, u32[]{:S(2)}, u32[]{:S(2)}) %collective-permute-start.2) | collective-permute-done | bytes 1048608 | tf_op jit(solution)/shard_map/while/body/eval_jaxpr/ppermute | solution.py:24
  582.6 5.4 collective-permute-start
  602.8 263.3 %collective-permute-done.2 = bf16[2,256,8,128]{1,3,2,0:T(8,128)(2,1)S(1)} collective-permute-done((bf16[2,256,8,128]{1,3,2,0:T(8,128)(2,1)}, bf16[2,256,8,128]{1,3,2,0:T(8,128)(2,1)S(1)}, u32[]{:S(2)}, u32[]{:S(2)}) %collective-permute-start.2) | collective-permute-done | bytes 1048608 | tf_op jit(solution)/shard_map/while/body/eval_jaxpr/ppermute | solution.py:24
  869.2 6.7 collective-permute-start
  880.7 20.9 %conditional.3 = (bf16[2,256,8,128]{1,3,2,0:T(8,128)(2,1)}, f32[9,256,256]{1,2,0:T(8,128)}) conditional(s32[]{:T(128)} %convert_element_type.29, () %tuple.63, (bf16[2,256,8,128]{1,3,2,0:T(8,128)(2,1)S(1)}, bf16[2,256,10,128]{1,3,2,0:T(8,128)(2,1)S(1)}, bf16[9,256,256]{2,1,0:T(8,128)(2,1)}, f32[2,256,8,128]{1,3,2,0:T(8,128)S(1)}, ...), branch_computations={%region_1.1_spmd, %region_2.2_spmd} | conditional | flops 4838129664 | bytes 100286512 | solution.py:93
  902.8 2.8 select_select_fusion.2
  908.1 15.6 %collective-permute-done.2 = bf16[2,256,8,128]{1,3,2,0:T(8,128)(2,1)S(1)} collective-permute-done((bf16[2,256,8,128]{1,3,2,0:T(8,128)(2,1)}, bf16[2,256,8,128]{1,3,2,0:T(8,128)(2,1)S(1)}, u32[]{:S(2)}, u32[]{:S(2)}) %collective-permute-start.2) | collective-permute-done | bytes 1048608 | tf_op jit(solution)/shard_map/while/body/eval_jaxpr/ppermute | solution.py:24
  931.0 148.6 %all-reduce.14.cloned.1.call-done = f32[1,9,256,256]{3,2,1,0:T(8,128)} async-done(((f32[1,9,256,256]{3,2,1,0:T(8,128)}), f32[1,9,256,256]{3,2,1,0:T(8,128)}) %all-reduce.14.cloned.1.call-update) | async-done | bytes 2359312 | tf_op jit(solution)/shard_map/psum | solution.py:111
  1079.6 3.2 copy.79
  (365 shorter events, 321.2 us)
Async XLA Ops:
  7.2 1072.4 %all-reduce.14.cloned.1.call-start = ((), (), s32[]{:S(2)}) async-start(), calls=%async_computation | async-start | bytes 4718592 | tf_op jit(solution)/shard_map/psum | solution.py:111
  10.8 8.8 collective-permute-start.3
  15.2 7.3 collective-permute-start.4
  25.8 6.1 collective-permute-start
  27.1 4.8 collective-permute-start.1
  35.8 19.6 %collective-permute-start.2 = (bf16[2,256,8,128]{1,3,2,0:T(8,128)(2,1)}, bf16[2,256,8,128]{1,3,2,0:T(8,128)(2,1)S(1)}, u32[]{:S(2)}, u32[]{:S(2)}) collective-permute-start(bf16[2,256,8,128]{1,3,2,0:T(8,128)(2,1)} %get-tuple-element.335), channel_id=1, source_target_pairs={{16,0},{32,16},{48,32},{64,48},{80,64},{96,80},{112,96},{128,112},... | collective-permute-start | bytes 3145736 | tf_op jit(solution)/shard_map/while/body/eval_jaxpr/ppermute | solution.py:24
  58.4 12.7 %collective-permute-start = (bf16[2,256,1,128]{1,3,2,0:T(8,128)(2,1)}, bf16[2,256,1,128]{1,3,2,0:T(8,128)(2,1)S(1)}, u32[]{:S(2)}, u32[]{:S(2)}) collective-permute-start(bf16[2,256,1,128]{1,3,2,0:T(8,128)(2,1)} %get-tuple-element.333), channel_id=1, source_target_pairs={{1,0},{2,1},{3,2},{4,3},{5,4},{6,5},{7,6},{8,7},{9,8},{10,9},{11,1... | collective-permute-start | bytes 393224 | tf_op jit(solution)/shard_map/while/body/eval_jaxpr/ppermute | solution.py:16
  66.4 5.5 collective-permute-start.1
  75.8 19.6 %collective-permute-start.2 = (bf16[2,256,8,128]{1,3,2,0:T(8,128)(2,1)}, bf16[2,256,8,128]{1,3,2,0:T(8,128)(2,1)S(1)}, u32[]{:S(2)}, u32[]{:S(2)}) collective-permute-start(bf16[2,256,8,128]{1,3,2,0:T(8,128)(2,1)} %get-tuple-element.335), channel_id=1, source_target_pairs={{16,0},{32,16},{48,32},{64,48},{80,64},{96,80},{112,96},{128,112},... | collective-permute-start | bytes 3145736 | tf_op jit(solution)/shard_map/while/body/eval_jaxpr/ppermute | solution.py:24
  98.4 12.1 %collective-permute-start = (bf16[2,256,1,128]{1,3,2,0:T(8,128)(2,1)}, bf16[2,256,1,128]{1,3,2,0:T(8,128)(2,1)S(1)}, u32[]{:S(2)}, u32[]{:S(2)}) collective-permute-start(bf16[2,256,1,128]{1,3,2,0:T(8,128)(2,1)} %get-tuple-element.333), channel_id=1, source_target_pairs={{1,0},{2,1},{3,2},{4,3},{5,4},{6,5},{7,6},{8,7},{9,8},{10,9},{11,1... | collective-permute-start | bytes 393224 | tf_op jit(solution)/shard_map/while/body/eval_jaxpr/ppermute | solution.py:16
  106.5 5.7 collective-permute-start.1
  115.9 20.5 %collective-permute-start.2 = (bf16[2,256,8,128]{1,3,2,0:T(8,128)(2,1)}, bf16[2,256,8,128]{1,3,2,0:T(8,128)(2,1)S(1)}, u32[]{:S(2)}, u32[]{:S(2)}) collective-permute-start(bf16[2,256,8,128]{1,3,2,0:T(8,128)(2,1)} %get-tuple-element.335), channel_id=1, source_target_pairs={{16,0},{32,16},{48,32},{64,48},{80,64},{96,80},{112,96},{128,112},... | collective-permute-start | bytes 3145736 | tf_op jit(solution)/shard_map/while/body/eval_jaxpr/ppermute | solution.py:24
  139.4 13.3 %collective-permute-start = (bf16[2,256,1,128]{1,3,2,0:T(8,128)(2,1)}, bf16[2,256,1,128]{1,3,2,0:T(8,128)(2,1)S(1)}, u32[]{:S(2)}, u32[]{:S(2)}) collective-permute-start(bf16[2,256,1,128]{1,3,2,0:T(8,128)(2,1)} %get-tuple-element.333), channel_id=1, source_target_pairs={{1,0},{2,1},{3,2},{4,3},{5,4},{6,5},{7,6},{8,7},{9,8},{10,9},{11,1... | collective-permute-start | bytes 393224 | tf_op jit(solution)/shard_map/while/body/eval_jaxpr/ppermute | solution.py:16
  147.2 6.3 collective-permute-start.1
  157.3 20.8 %collective-permute-start.2 = (bf16[2,256,8,128]{1,3,2,0:T(8,128)(2,1)}, bf16[2,256,8,128]{1,3,2,0:T(8,128)(2,1)S(1)}, u32[]{:S(2)}, u32[]{:S(2)}) collective-permute-start(bf16[2,256,8,128]{1,3,2,0:T(8,128)(2,1)} %get-tuple-element.335), channel_id=1, source_target_pairs={{16,0},{32,16},{48,32},{64,48},{80,64},{96,80},{112,96},{128,112},... | collective-permute-start | bytes 3145736 | tf_op jit(solution)/shard_map/while/body/eval_jaxpr/ppermute | solution.py:24
  181.1 13.4 %collective-permute-start = (bf16[2,256,1,128]{1,3,2,0:T(8,128)(2,1)}, bf16[2,256,1,128]{1,3,2,0:T(8,128)(2,1)S(1)}, u32[]{:S(2)}, u32[]{:S(2)}) collective-permute-start(bf16[2,256,1,128]{1,3,2,0:T(8,128)(2,1)} %get-tuple-element.333), channel_id=1, source_target_pairs={{1,0},{2,1},{3,2},{4,3},{5,4},{6,5},{7,6},{8,7},{9,8},{10,9},{11,1... | collective-permute-start | bytes 393224 | tf_op jit(solution)/shard_map/while/body/eval_jaxpr/ppermute | solution.py:16
  188.0 7.3 collective-permute-start.1
  199.1 23.6 %collective-permute-start.2 = (bf16[2,256,8,128]{1,3,2,0:T(8,128)(2,1)}, bf16[2,256,8,128]{1,3,2,0:T(8,128)(2,1)S(1)}, u32[]{:S(2)}, u32[]{:S(2)}) collective-permute-start(bf16[2,256,8,128]{1,3,2,0:T(8,128)(2,1)} %get-tuple-element.335), channel_id=1, source_target_pairs={{16,0},{32,16},{48,32},{64,48},{80,64},{96,80},{112,96},{128,112},... | collective-permute-start | bytes 3145736 | tf_op jit(solution)/shard_map/while/body/eval_jaxpr/ppermute | solution.py:24
  225.7 9.5 collective-permute-start
  229.8 5.4 collective-permute-start.1
  239.0 23.7 %collective-permute-start.2 = (bf16[2,256,8,128]{1,3,2,0:T(8,128)(2,1)}, bf16[2,256,8,128]{1,3,2,0:T(8,128)(2,1)S(1)}, u32[]{:S(2)}, u32[]{:S(2)}) collective-permute-start(bf16[2,256,8,128]{1,3,2,0:T(8,128)(2,1)} %get-tuple-element.335), channel_id=1, source_target_pairs={{16,0},{32,16},{48,32},{64,48},{80,64},{96,80},{112,96},{128,112},... | collective-permute-start | bytes 3145736 | tf_op jit(solution)/shard_map/while/body/eval_jaxpr/ppermute | solution.py:24
  265.8 8.8 collective-permute-start
  270.0 4.6 collective-permute-start.1
  278.4 23.0 %collective-permute-start.2 = (bf16[2,256,8,128]{1,3,2,0:T(8,128)(2,1)}, bf16[2,256,8,128]{1,3,2,0:T(8,128)(2,1)S(1)}, u32[]{:S(2)}, u32[]{:S(2)}) collective-permute-start(bf16[2,256,8,128]{1,3,2,0:T(8,128)(2,1)} %get-tuple-element.335), channel_id=1, source_target_pairs={{16,0},{32,16},{48,32},{64,48},{80,64},{96,80},{112,96},{128,112},... | collective-permute-start | bytes 3145736 | tf_op jit(solution)/shard_map/while/body/eval_jaxpr/ppermute | solution.py:24
  304.4 9.4 collective-permute-start
  309.3 4.5 collective-permute-start.1
  317.6 22.9 %collective-permute-start.2 = (bf16[2,256,8,128]{1,3,2,0:T(8,128)(2,1)}, bf16[2,256,8,128]{1,3,2,0:T(8,128)(2,1)S(1)}, u32[]{:S(2)}, u32[]{:S(2)}) collective-permute-start(bf16[2,256,8,128]{1,3,2,0:T(8,128)(2,1)} %get-tuple-element.335), channel_id=1, source_target_pairs={{16,0},{32,16},{48,32},{64,48},{80,64},{96,80},{112,96},{128,112},... | collective-permute-start | bytes 3145736 | tf_op jit(solution)/shard_map/while/body/eval_jaxpr/ppermute | solution.py:24
  343.5 9.4 collective-permute-start
  348.6 4.3 collective-permute-start.1
  356.7 22.7 %collective-permute-start.2 = (bf16[2,256,8,128]{1,3,2,0:T(8,128)(2,1)}, bf16[2,256,8,128]{1,3,2,0:T(8,128)(2,1)S(1)}, u32[]{:S(2)}, u32[]{:S(2)}) collective-permute-start(bf16[2,256,8,128]{1,3,2,0:T(8,128)(2,1)} %get-tuple-element.335), channel_id=1, source_target_pairs={{16,0},{32,16},{48,32},{64,48},{80,64},{96,80},{112,96},{128,112},... | collective-permute-start | bytes 3145736 | tf_op jit(solution)/shard_map/while/body/eval_jaxpr/ppermute | solution.py:24
  382.5 9.4 collective-permute-start
  395.7 22.7 %collective-permute-start.2 = (bf16[2,256,8,128]{1,3,2,0:T(8,128)(2,1)}, bf16[2,256,8,128]{1,3,2,0:T(8,128)(2,1)S(1)}, u32[]{:S(2)}, u32[]{:S(2)}) collective-permute-start(bf16[2,256,8,128]{1,3,2,0:T(8,128)(2,1)} %get-tuple-element.335), channel_id=1, source_target_pairs={{16,0},{32,16},{48,32},{64,48},{80,64},{96,80},{112,96},{128,112},... | collective-permute-start | bytes 3145736 | tf_op jit(solution)/shard_map/while/body/eval_jaxpr/ppermute | solution.py:24
  421.5 9.6 collective-permute-start
  434.8 23.9 %collective-permute-start.2 = (bf16[2,256,8,128]{1,3,2,0:T(8,128)(2,1)}, bf16[2,256,8,128]{1,3,2,0:T(8,128)(2,1)S(1)}, u32[]{:S(2)}, u32[]{:S(2)}) collective-permute-start(bf16[2,256,8,128]{1,3,2,0:T(8,128)(2,1)} %get-tuple-element.335), channel_id=1, source_target_pairs={{16,0},{32,16},{48,32},{64,48},{80,64},{96,80},{112,96},{128,112},... | collective-permute-start | bytes 3145736 | tf_op jit(solution)/shard_map/while/body/eval_jaxpr/ppermute | solution.py:24
  461.8 10.2 collective-permute-start
  467.2 4.8 collective-permute-start.1
  475.8 23.4 %collective-permute-start.2 = (bf16[2,256,8,128]{1,3,2,0:T(8,128)(2,1)}, bf16[2,256,8,128]{1,3,2,0:T(8,128)(2,1)S(1)}, u32[]{:S(2)}, u32[]{:S(2)}) collective-permute-start(bf16[2,256,8,128]{1,3,2,0:T(8,128)(2,1)} %get-tuple-element.335), channel_id=1, source_target_pairs={{16,0},{32,16},{48,32},{64,48},{80,64},{96,80},{112,96},{128,112},... | collective-permute-start | bytes 3145736 | tf_op jit(solution)/shard_map/while/body/eval_jaxpr/ppermute | solution.py:24
  502.2 10.2 collective-permute-start
  507.6 4.8 collective-permute-start.1
  516.2 23.3 %collective-permute-start.2 = (bf16[2,256,8,128]{1,3,2,0:T(8,128)(2,1)}, bf16[2,256,8,128]{1,3,2,0:T(8,128)(2,1)S(1)}, u32[]{:S(2)}, u32[]{:S(2)}) collective-permute-start(bf16[2,256,8,128]{1,3,2,0:T(8,128)(2,1)} %get-tuple-element.335), channel_id=1, source_target_pairs={{16,0},{32,16},{48,32},{64,48},{80,64},{96,80},{112,96},{128,112},... | collective-permute-start | bytes 3145736 | tf_op jit(solution)/shard_map/while/body/eval_jaxpr/ppermute | solution.py:24
  542.5 10.2 collective-permute-start
  547.9 4.8 collective-permute-start.1
  556.5 23.1 %collective-permute-start.2 = (bf16[2,256,8,128]{1,3,2,0:T(8,128)(2,1)}, bf16[2,256,8,128]{1,3,2,0:T(8,128)(2,1)S(1)}, u32[]{:S(2)}, u32[]{:S(2)}) collective-permute-start(bf16[2,256,8,128]{1,3,2,0:T(8,128)(2,1)} %get-tuple-element.335), channel_id=1, source_target_pairs={{16,0},{32,16},{48,32},{64,48},{80,64},{96,80},{112,96},{128,112},... | collective-permute-start | bytes 3145736 | tf_op jit(solution)/shard_map/while/body/eval_jaxpr/ppermute | solution.py:24
  582.6 10.2 collective-permute-start
  587.9 4.8 collective-permute-start.1
  596.5 269.6 %collective-permute-start.2 = (bf16[2,256,8,128]{1,3,2,0:T(8,128)(2,1)}, bf16[2,256,8,128]{1,3,2,0:T(8,128)(2,1)S(1)}, u32[]{:S(2)}, u32[]{:S(2)}) collective-permute-start(bf16[2,256,8,128]{1,3,2,0:T(8,128)(2,1)} %get-tuple-element.335), channel_id=1, source_target_pairs={{16,0},{32,16},{48,32},{64,48},{80,64},{96,80},{112,96},{128,112},... | collective-permute-start | bytes 3145736 | tf_op jit(solution)/shard_map/while/body/eval_jaxpr/ppermute | solution.py:24
  869.2 10.4 collective-permute-start
  901.5 22.1 %collective-permute-start.2 = (bf16[2,256,8,128]{1,3,2,0:T(8,128)(2,1)}, bf16[2,256,8,128]{1,3,2,0:T(8,128)(2,1)S(1)}, u32[]{:S(2)}, u32[]{:S(2)}) collective-permute-start(bf16[2,256,8,128]{1,3,2,0:T(8,128)(2,1)} %get-tuple-element.335), channel_id=1, source_target_pairs={{16,0},{32,16},{48,32},{64,48},{80,64},{96,80},{112,96},{128,112},... | collective-permute-start | bytes 3145736 | tf_op jit(solution)/shard_map/while/body/eval_jaxpr/ppermute | solution.py:24
  (70 other events, 630.7 us)
Sparse Core Ops, SparseCore 0:
  928.4 151.1 all-reduce.13
where the time goes:
time: 1090 us
  waiting for transfers between devices  686 us (63%)
  starting transfers between devices  144 us (13%)
  other arithmetic  122 us (11%)
  local copies, waits for them, and re-layouts  95 us (9%)
  matrix products  17.4 us (2%)
  between operations  14.1 us (1%)
  loops' own time  11.6 us (1%)
    ppermute x16, waiting for transfers between devices, from_behind(): return lax.ppermute(block, axis, route)  504 us
    psum x1, waiting for transfers between devices, per_device(): weight_grad = lax.psum(kernel_acc * scale, 'tile')  149 us
    ppermute x17, starting transfers between devices, padded_2(): lax.ppermute(lax.slice_in_dim(block, 0, width, axis=dim), axis, backward)  89.3 us
    another operation x31, local copies, waits for them, and re-layouts  41.5 us
    add x16, other arithmetic, one_tick(): kernel_acc = kernel_acc + partial_k  39.1 us
    select_n x16, other arithmetic, one_tick(): grads = jnp.where(valid, lowered, old_grads)  39 us
    ppermute x17, starting transfers between devices, padded_2(): lax.ppermute(lax.slice_in_dim(block, block.shape[dim] - width, None, axis...  33.7 us
    ppermute x17, waiting for transfers between devices, padded_2(): lax.ppermute(lax.slice_in_dim(block, 0, width, axis=dim), axis, backward)  28.9 us
  transfers between devices with their start and end apart: 51, of which 39 were waited for; matrix products, arithmetic and copies ran while one was open for 9% of the time, Pallas kernels for 0%

commit v1 on v0

--- a/solution.py
+++ b/solution.py
@@ -108,7 +108,7 @@
     final, unused = lax.scan(one_tick, initial, jnp.arange(ticks, dtype=jnp.int32))
     grads = final[1]
     kernel_acc = final[2]
-    weight_grad = lax.psum(kernel_acc * scale, "tile")
+    weight_grad = jnp.sum(lax.all_gather(kernel_acc * scale, "tile"), axis=0)
     return (grads[None], weight_grad[None])
 
 

time: 1090 us -> 1170 us (1.073)
  waiting for transfers between devices: 686 us -> 750 us
  other arithmetic: 122 us -> 135 us
    all_gather x0 -> x1, waiting for transfers between devices: none -> 211 us  [per_device(): weight_grad = jnp.sum(lax.all_gather(kernel_acc * scale, 'tile'), axis=0)]
    psum x1 -> x0, waiting for transfers between devices: 149 us -> none  [per_device(): weight_grad = lax.psum(kernel_acc * scale, 'tile')]
    reduce_sum x0 -> x1, other arithmetic: none -> 14.9 us  [per_device(): weight_grad = jnp.sum(lax.all_gather(kernel_acc * scale, 'tile'), axis=0)]
  transfers between devices with their start and end apart: 51 -> 51, of which waited for: 39 -> 39; matrix products, arithmetic and copies ran while one was open for 9% -> 8% of each run, Pallas kernels for 0% -> 0%
where the time goes in v1:
time: 1170 us
  waiting for transfers between devices  750 us (64%)
  starting transfers between devices  143 us (12%)
  other arithmetic  135 us (12%)
  local copies, waits for them, and re-layouts  97.4 us (8%)
  matrix products  17.4 us (1%)
  between operations  14.1 us (1%)
  loops' own time  12.5 us (1%)
    ppermute x16, waiting for transfers between devices, from_behind(): return lax.ppermute(block, axis, route)  507 us
    all_gather x1, waiting for transfers between devices, per_device(): weight_grad = jnp.sum(lax.all_gather(kernel_acc * scale, 'tile'), axis=0)  211 us
    ppermute x17, starting transfers between devices, padded_2(): lax.ppermute(lax.slice_in_dim(block, 0, width, axis=dim), axis, backward)  89.4 us
    another operation x31, local copies, waits for them, and re-layouts  41.6 us
    add x16, other arithmetic, one_tick(): kernel_acc = kernel_acc + partial_k  39.1 us
    select_n x16, other arithmetic, one_tick(): grads = jnp.where(valid, lowered, old_grads)  38.8 us
    ppermute x17, starting transfers between devices, padded_2(): lax.ppermute(lax.slice_in_dim(block, block.shape[dim] - width, None, axis...  33.5 us
    ppermute x17, waiting for transfers between devices, padded_2(): lax.ppermute(lax.slice_in_dim(block, 0, width, axis=dim), axis, backward)  27.5 us
  transfers between devices with their start and end apart: 51, of which 39 were waited for; matrix products, arithmetic and copies ran while one was open for 8% of the time, Pallas kernels for 0%

profile of v1, /device:TPU:1, one launch (start us, length us, event | category | flops | bytes accessed | tf_op | source)
XLA Modules:
  0.0 1170.3 jit_solution(12365275682039466058)
XLA Ops:
  10.0 4.3 collective-permute-start.3
  18.6 3.0 collective-permute-done.4
  22.9 904.1 %while.17 = (s32[]{:T(128)}, bf16[2,256,8,128]{1,3,2,0:T(8,128)(2,1)}, bf16[2,256,8,128]{1,3,2,0:T(8,128)(2,1)}, f32[9,256,256]{1,2,0:T(8,128)}, s32[16]{0:T(128...) while((s32[]{:T(128)}, ...), condition=%wide.region_3.4_spmd.clone, body=%wide.region_0.3_spmd.clone.sunk | while | flops 4842192896 | bytes 153502240 | solution.py:108
  32.2 2.7 conditional.3
  40.7 13.8 %collective-permute-done.2 = bf16[2,256,8,128]{1,3,2,0:T(8,128)(2,1)S(1)} collective-permute-done((bf16[2,256,8,128]{1,3,2,0:T(8,128)(2,1)}, bf16[2,256,8,128]{1,3,2,0:T(8,128)(2,1)S(1)}, u32[]{:S(2)}, u32[]{:S(2)}) %collective-permute-start.2) | collective-permute-done | bytes 1048608 | tf_op jit(solution)/shard_map/while/body/eval_jaxpr/ppermute | solution.py:24
  57.5 8.1 collective-permute-start
  72.2 2.7 conditional.3
  81.2 13.3 %collective-permute-done.2 = bf16[2,256,8,128]{1,3,2,0:T(8,128)(2,1)S(1)} collective-permute-done((bf16[2,256,8,128]{1,3,2,0:T(8,128)(2,1)}, bf16[2,256,8,128]{1,3,2,0:T(8,128)(2,1)S(1)}, u32[]{:S(2)}, u32[]{:S(2)}) %collective-permute-start.2) | collective-permute-done | bytes 1048608 | tf_op jit(solution)/shard_map/while/body/eval_jaxpr/ppermute | solution.py:24
  97.6 8.1 collective-permute-start
  112.4 2.7 conditional.3
  121.3 14.2 %collective-permute-done.2 = bf16[2,256,8,128]{1,3,2,0:T(8,128)(2,1)S(1)} collective-permute-done((bf16[2,256,8,128]{1,3,2,0:T(8,128)(2,1)}, bf16[2,256,8,128]{1,3,2,0:T(8,128)(2,1)S(1)}, u32[]{:S(2)}, u32[]{:S(2)}) %collective-permute-start.2) | collective-permute-done | bytes 1048608 | tf_op jit(solution)/shard_map/while/body/eval_jaxpr/ppermute | solution.py:24
  138.6 7.8 collective-permute-start
  153.7 2.7 conditional.3
  162.7 14.4 %collective-permute-done.2 = bf16[2,256,8,128]{1,3,2,0:T(8,128)(2,1)S(1)} collective-permute-done((bf16[2,256,8,128]{1,3,2,0:T(8,128)(2,1)}, bf16[2,256,8,128]{1,3,2,0:T(8,128)(2,1)S(1)}, u32[]{:S(2)}, u32[]{:S(2)}) %collective-permute-start.2) | collective-permute-done | bytes 1048608 | tf_op jit(solution)/shard_map/while/body/eval_jaxpr/ppermute | solution.py:24
  180.1 7.0 collective-permute-start
  187.1 3.7 collective-permute-start.1
  195.5 2.7 conditional.3
  204.4 17.3 %collective-permute-done.2 = bf16[2,256,8,128]{1,3,2,0:T(8,128)(2,1)S(1)} collective-permute-done((bf16[2,256,8,128]{1,3,2,0:T(8,128)(2,1)}, bf16[2,256,8,128]{1,3,2,0:T(8,128)(2,1)S(1)}, u32[]{:S(2)}, u32[]{:S(2)}) %collective-permute-start.2) | collective-permute-done | bytes 1048608 | tf_op jit(solution)/shard_map/while/body/eval_jaxpr/ppermute | solution.py:24
  224.8 4.2 collective-permute-start
  244.4 17.5 %collective-permute-done.2 = bf16[2,256,8,128]{1,3,2,0:T(8,128)(2,1)S(1)} collective-permute-done((bf16[2,256,8,128]{1,3,2,0:T(8,128)(2,1)}, bf16[2,256,8,128]{1,3,2,0:T(8,128)(2,1)S(1)}, u32[]{:S(2)}, u32[]{:S(2)}) %collective-permute-start.2) | collective-permute-done | bytes 1048608 | tf_op jit(solution)/shard_map/while/body/eval_jaxpr/ppermute | solution.py:24
  264.9 4.2 collective-permute-start
  283.7 16.7 %collective-permute-done.2 = bf16[2,256,8,128]{1,3,2,0:T(8,128)(2,1)S(1)} collective-permute-done((bf16[2,256,8,128]{1,3,2,0:T(8,128)(2,1)}, bf16[2,256,8,128]{1,3,2,0:T(8,128)(2,1)S(1)}, u32[]{:S(2)}, u32[]{:S(2)}) %collective-permute-start.2) | collective-permute-done | bytes 1048608 | tf_op jit(solution)/shard_map/while/body/eval_jaxpr/ppermute | solution.py:24
  303.5 5.0 collective-permute-start
  314.0 2.7 conditional.3
  323.0 16.6 %collective-permute-done.2 = bf16[2,256,8,128]{1,3,2,0:T(8,128)(2,1)S(1)} collective-permute-done((bf16[2,256,8,128]{1,3,2,0:T(8,128)(2,1)}, bf16[2,256,8,128]{1,3,2,0:T(8,128)(2,1)S(1)}, u32[]{:S(2)}, u32[]{:S(2)}) %collective-permute-start.2) | collective-permute-done | bytes 1048608 | tf_op jit(solution)/shard_map/while/body/eval_jaxpr/ppermute | solution.py:24
  342.6 5.1 collective-permute-start
  362.1 16.5 %collective-permute-done.2 = bf16[2,256,8,128]{1,3,2,0:T(8,128)(2,1)S(1)} collective-permute-done((bf16[2,256,8,128]{1,3,2,0:T(8,128)(2,1)}, bf16[2,256,8,128]{1,3,2,0:T(8,128)(2,1)S(1)}, u32[]{:S(2)}, u32[]{:S(2)}) %collective-permute-start.2) | collective-permute-done | bytes 1048608 | tf_op jit(solution)/shard_map/while/body/eval_jaxpr/ppermute | solution.py:24
  381.6 5.2 collective-permute-start
  392.2 2.7 conditional.3
  401.1 16.5 %collective-permute-done.2 = bf16[2,256,8,128]{1,3,2,0:T(8,128)(2,1)S(1)} collective-permute-done((bf16[2,256,8,128]{1,3,2,0:T(8,128)(2,1)}, bf16[2,256,8,128]{1,3,2,0:T(8,128)(2,1)S(1)}, u32[]{:S(2)}, u32[]{:S(2)}) %collective-permute-start.2) | collective-permute-done | bytes 1048608 | tf_op jit(solution)/shard_map/while/body/eval_jaxpr/ppermute | solution.py:24
  420.6 5.4 collective-permute-start
  440.3 17.7 %collective-permute-done.2 = bf16[2,256,8,128]{1,3,2,0:T(8,128)(2,1)S(1)} collective-permute-done((bf16[2,256,8,128]{1,3,2,0:T(8,128)(2,1)}, bf16[2,256,8,128]{1,3,2,0:T(8,128)(2,1)S(1)}, u32[]{:S(2)}, u32[]{:S(2)}) %collective-permute-start.2) | collective-permute-done | bytes 1048608 | tf_op jit(solution)/shard_map/while/body/eval_jaxpr/ppermute | solution.py:24
  461.0 5.4 collective-permute-start
  481.2 17.2 %collective-permute-done.2 = bf16[2,256,8,128]{1,3,2,0:T(8,128)(2,1)S(1)} collective-permute-done((bf16[2,256,8,128]{1,3,2,0:T(8,128)(2,1)}, bf16[2,256,8,128]{1,3,2,0:T(8,128)(2,1)S(1)}, u32[]{:S(2)}, u32[]{:S(2)}) %collective-permute-start.2) | collective-permute-done | bytes 1048608 | tf_op jit(solution)/shard_map/while/body/eval_jaxpr/ppermute | solution.py:24
  501.4 5.4 collective-permute-start
  512.7 2.7 conditional.3
  521.7 17.0 %collective-permute-done.2 = bf16[2,256,8,128]{1,3,2,0:T(8,128)(2,1)S(1)} collective-permute-done((bf16[2,256,8,128]{1,3,2,0:T(8,128)(2,1)}, bf16[2,256,8,128]{1,3,2,0:T(8,128)(2,1)S(1)}, u32[]{:S(2)}, u32[]{:S(2)}) %collective-permute-start.2) | collective-permute-done | bytes 1048608 | tf_op jit(solution)/shard_map/while/body/eval_jaxpr/ppermute | solution.py:24
  541.7 5.4 collective-permute-start
  562.0 16.8 %collective-permute-done.2 = bf16[2,256,8,128]{1,3,2,0:T(8,128)(2,1)S(1)} collective-permute-done((bf16[2,256,8,128]{1,3,2,0:T(8,128)(2,1)}, bf16[2,256,8,128]{1,3,2,0:T(8,128)(2,1)S(1)}, u32[]{:S(2)}, u32[]{:S(2)}) %collective-permute-start.2) | collective-permute-done | bytes 1048608 | tf_op jit(solution)/shard_map/while/body/eval_jaxpr/ppermute | solution.py:24
  581.8 5.4 collective-permute-start
  593.0 2.7 conditional.3
  602.0 266.2 %collective-permute-done.2 = bf16[2,256,8,128]{1,3,2,0:T(8,128)(2,1)S(1)} collective-permute-done((bf16[2,256,8,128]{1,3,2,0:T(8,128)(2,1)}, bf16[2,256,8,128]{1,3,2,0:T(8,128)(2,1)S(1)}, u32[]{:S(2)}, u32[]{:S(2)}) %collective-permute-start.2) | collective-permute-done | bytes 1048608 | tf_op jit(solution)/shard_map/while/body/eval_jaxpr/ppermute | solution.py:24
  871.2 6.7 collective-permute-start
  882.8 21.1 %conditional.3 = (bf16[2,256,8,128]{1,3,2,0:T(8,128)(2,1)}, f32[9,256,256]{1,2,0:T(8,128)}) conditional(s32[]{:T(128)} %convert_element_type.29, () %tuple.65, (bf16[2,256,8,128]{1,3,2,0:T(8,128)(2,1)S(1)}, bf16[2,256,10,128]{1,3,2,0:T(8,128)(2,1)S(1)}, bf16[9,256,256]{2,1,0:T(8,128)(2,1)}, f32[2,256,8,128]{1,3,2,0:T(8,128)S(1)}, ...), branch_computations={%region_1.1_spmd, %region_2.2_spmd} | conditional | flops 4838129664 | bytes 100286512 | solution.py:93
  905.1 2.8 select_select_fusion.2
  910.4 15.6 %collective-permute-done.2 = bf16[2,256,8,128]{1,3,2,0:T(8,128)(2,1)S(1)} collective-permute-done((bf16[2,256,8,128]{1,3,2,0:T(8,128)(2,1)}, bf16[2,256,8,128]{1,3,2,0:T(8,128)(2,1)S(1)}, u32[]{:S(2)}, u32[]{:S(2)}) %collective-permute-start.2) | collective-permute-done | bytes 1048608 | tf_op jit(solution)/shard_map/while/body/eval_jaxpr/ppermute | solution.py:24
  933.3 211.2 %all-gather.3.cloned.1.call-done = f32[144,256,256]{2,1,0:T(8,128)} async-done(((f32[9,256,256]{2,1,0:T(8,128)}), f32[144,256,256]{2,1,0:T(8,128)}) %all-gather.3.cloned.1.call-update) | async-done | bytes 37748752 | tf_op jit(solution)/shard_map/all_gather | solution.py:111
  1144.5 14.9 %reduce_sum.9 = f32[9,256,256]{2,1,0:T(8,128)} reduce(f32[16,9,256,256]{3,2,1,0:T(8,128)} %bitcast.173, f32[]{:T(128)} %constant.33.clone.1), dimensions={0}, to_apply=%region_4.5 | reduce | flops 8847360 | bytes 40108036 | tf_op jit(solution)/shard_map/reduce_sum | solution.py:111
  (365 shorter events, 324.7 us)
Async XLA Ops:
  7.2 1137.4 %all-gather.3.cloned.1.call-start = ((), (), s32[]{:S(2)}) async-start(), calls=%async_computation | async-start | bytes 40108032 | tf_op jit(solution)/shard_map/all_gather | solution.py:111
  10.0 8.6 collective-permute-start.3
  14.3 7.3 collective-permute-start.4
  24.9 6.1 collective-permute-start
  26.2 4.9 collective-permute-start.1
  34.9 19.6 %collective-permute-start.2 = (bf16[2,256,8,128]{1,3,2,0:T(8,128)(2,1)}, bf16[2,256,8,128]{1,3,2,0:T(8,128)(2,1)S(1)}, u32[]{:S(2)}, u32[]{:S(2)}) collective-permute-start(bf16[2,256,8,128]{1,3,2,0:T(8,128)(2,1)} %get-tuple-element.349), channel_id=1, source_target_pairs={{16,0},{32,16},{48,32},{64,48},{80,64},{96,80},{112,96},{128,112},... | collective-permute-start | bytes 3145736 | tf_op jit(solution)/shard_map/while/body/eval_jaxpr/ppermute | solution.py:24
  57.5 12.7 %collective-permute-start = (bf16[2,256,1,128]{1,3,2,0:T(8,128)(2,1)}, bf16[2,256,1,128]{1,3,2,0:T(8,128)(2,1)S(1)}, u32[]{:S(2)}, u32[]{:S(2)}) collective-permute-start(bf16[2,256,1,128]{1,3,2,0:T(8,128)(2,1)} %get-tuple-element.347), channel_id=1, source_target_pairs={{1,0},{2,1},{3,2},{4,3},{5,4},{6,5},{7,6},{8,7},{9,8},{10,9},{11,1... | collective-permute-start | bytes 393224 | tf_op jit(solution)/shard_map/while/body/eval_jaxpr/ppermute | solution.py:16
  65.6 5.5 collective-permute-start.1
  74.9 19.6 %collective-permute-start.2 = (bf16[2,256,8,128]{1,3,2,0:T(8,128)(2,1)}, bf16[2,256,8,128]{1,3,2,0:T(8,128)(2,1)S(1)}, u32[]{:S(2)}, u32[]{:S(2)}) collective-permute-start(bf16[2,256,8,128]{1,3,2,0:T(8,128)(2,1)} %get-tuple-element.349), channel_id=1, source_target_pairs={{16,0},{32,16},{48,32},{64,48},{80,64},{96,80},{112,96},{128,112},... | collective-permute-start | bytes 3145736 | tf_op jit(solution)/shard_map/while/body/eval_jaxpr/ppermute | solution.py:24
  97.6 12.0 %collective-permute-start = (bf16[2,256,1,128]{1,3,2,0:T(8,128)(2,1)}, bf16[2,256,1,128]{1,3,2,0:T(8,128)(2,1)S(1)}, u32[]{:S(2)}, u32[]{:S(2)}) collective-permute-start(bf16[2,256,1,128]{1,3,2,0:T(8,128)(2,1)} %get-tuple-element.347), channel_id=1, source_target_pairs={{1,0},{2,1},{3,2},{4,3},{5,4},{6,5},{7,6},{8,7},{9,8},{10,9},{11,1... | collective-permute-start | bytes 393224 | tf_op jit(solution)/shard_map/while/body/eval_jaxpr/ppermute | solution.py:16
  105.6 5.7 collective-permute-start.1
  115.1 20.5 %collective-permute-start.2 = (bf16[2,256,8,128]{1,3,2,0:T(8,128)(2,1)}, bf16[2,256,8,128]{1,3,2,0:T(8,128)(2,1)S(1)}, u32[]{:S(2)}, u32[]{:S(2)}) collective-permute-start(bf16[2,256,8,128]{1,3,2,0:T(8,128)(2,1)} %get-tuple-element.349), channel_id=1, source_target_pairs={{16,0},{32,16},{48,32},{64,48},{80,64},{96,80},{112,96},{128,112},... | collective-permute-start | bytes 3145736 | tf_op jit(solution)/shard_map/while/body/eval_jaxpr/ppermute | solution.py:24
  138.6 13.2 %collective-permute-start = (bf16[2,256,1,128]{1,3,2,0:T(8,128)(2,1)}, bf16[2,256,1,128]{1,3,2,0:T(8,128)(2,1)S(1)}, u32[]{:S(2)}, u32[]{:S(2)}) collective-permute-start(bf16[2,256,1,128]{1,3,2,0:T(8,128)(2,1)} %get-tuple-element.347), channel_id=1, source_target_pairs={{1,0},{2,1},{3,2},{4,3},{5,4},{6,5},{7,6},{8,7},{9,8},{10,9},{11,1... | collective-permute-start | bytes 393224 | tf_op jit(solution)/shard_map/while/body/eval_jaxpr/ppermute | solution.py:16
  146.3 6.3 collective-permute-start.1
  156.4 20.7 %collective-permute-start.2 = (bf16[2,256,8,128]{1,3,2,0:T(8,128)(2,1)}, bf16[2,256,8,128]{1,3,2,0:T(8,128)(2,1)S(1)}, u32[]{:S(2)}, u32[]{:S(2)}) collective-permute-start(bf16[2,256,8,128]{1,3,2,0:T(8,128)(2,1)} %get-tuple-element.349), channel_id=1, source_target_pairs={{16,0},{32,16},{48,32},{64,48},{80,64},{96,80},{112,96},{128,112},... | collective-permute-start | bytes 3145736 | tf_op jit(solution)/shard_map/while/body/eval_jaxpr/ppermute | solution.py:24
  180.1 13.5 %collective-permute-start = (bf16[2,256,1,128]{1,3,2,0:T(8,128)(2,1)}, bf16[2,256,1,128]{1,3,2,0:T(8,128)(2,1)S(1)}, u32[]{:S(2)}, u32[]{:S(2)}) collective-permute-start(bf16[2,256,1,128]{1,3,2,0:T(8,128)(2,1)} %get-tuple-element.347), channel_id=1, source_target_pairs={{1,0},{2,1},{3,2},{4,3},{5,4},{6,5},{7,6},{8,7},{9,8},{10,9},{11,1... | collective-permute-start | bytes 393224 | tf_op jit(solution)/shard_map/while/body/eval_jaxpr/ppermute | solution.py:16
  187.1 7.3 collective-permute-start.1
  198.2 23.6 %collective-permute-start.2 = (bf16[2,256,8,128]{1,3,2,0:T(8,128)(2,1)}, bf16[2,256,8,128]{1,3,2,0:T(8,128)(2,1)S(1)}, u32[]{:S(2)}, u32[]{:S(2)}) collective-permute-start(bf16[2,256,8,128]{1,3,2,0:T(8,128)(2,1)} %get-tuple-element.349), channel_id=1, source_target_pairs={{16,0},{32,16},{48,32},{64,48},{80,64},{96,80},{112,96},{128,112},... | collective-permute-start | bytes 3145736 | tf_op jit(solution)/shard_map/while/body/eval_jaxpr/ppermute | solution.py:24
  224.8 9.5 collective-permute-start
  229.0 5.4 collective-permute-start.1
  238.1 23.7 %collective-permute-start.2 = (bf16[2,256,8,128]{1,3,2,0:T(8,128)(2,1)}, bf16[2,256,8,128]{1,3,2,0:T(8,128)(2,1)S(1)}, u32[]{:S(2)}, u32[]{:S(2)}) collective-permute-start(bf16[2,256,8,128]{1,3,2,0:T(8,128)(2,1)} %get-tuple-element.349), channel_id=1, source_target_pairs={{16,0},{32,16},{48,32},{64,48},{80,64},{96,80},{112,96},{128,112},... | collective-permute-start | bytes 3145736 | tf_op jit(solution)/shard_map/while/body/eval_jaxpr/ppermute | solution.py:24
  264.9 8.8 collective-permute-start
  269.1 4.6 collective-permute-start.1
  277.5 23.0 %collective-permute-start.2 = (bf16[2,256,8,128]{1,3,2,0:T(8,128)(2,1)}, bf16[2,256,8,128]{1,3,2,0:T(8,128)(2,1)S(1)}, u32[]{:S(2)}, u32[]{:S(2)}) collective-permute-start(bf16[2,256,8,128]{1,3,2,0:T(8,128)(2,1)} %get-tuple-element.349), channel_id=1, source_target_pairs={{16,0},{32,16},{48,32},{64,48},{80,64},{96,80},{112,96},{128,112},... | collective-permute-start | bytes 3145736 | tf_op jit(solution)/shard_map/while/body/eval_jaxpr/ppermute | solution.py:24
  303.5 9.4 collective-permute-start
  308.5 4.5 collective-permute-start.1
  316.7 22.9 %collective-permute-start.2 = (bf16[2,256,8,128]{1,3,2,0:T(8,128)(2,1)}, bf16[2,256,8,128]{1,3,2,0:T(8,128)(2,1)S(1)}, u32[]{:S(2)}, u32[]{:S(2)}) collective-permute-start(bf16[2,256,8,128]{1,3,2,0:T(8,128)(2,1)} %get-tuple-element.349), channel_id=1, source_target_pairs={{16,0},{32,16},{48,32},{64,48},{80,64},{96,80},{112,96},{128,112},... | collective-permute-start | bytes 3145736 | tf_op jit(solution)/shard_map/while/body/eval_jaxpr/ppermute | solution.py:24
  342.6 9.4 collective-permute-start
  347.7 4.3 collective-permute-start.1
  355.9 22.7 %collective-permute-start.2 = (bf16[2,256,8,128]{1,3,2,0:T(8,128)(2,1)}, bf16[2,256,8,128]{1,3,2,0:T(8,128)(2,1)S(1)}, u32[]{:S(2)}, u32[]{:S(2)}) collective-permute-start(bf16[2,256,8,128]{1,3,2,0:T(8,128)(2,1)} %get-tuple-element.349), channel_id=1, source_target_pairs={{16,0},{32,16},{48,32},{64,48},{80,64},{96,80},{112,96},{128,112},... | collective-permute-start | bytes 3145736 | tf_op jit(solution)/shard_map/while/body/eval_jaxpr/ppermute | solution.py:24
  381.6 9.4 collective-permute-start
  394.9 22.7 %collective-permute-start.2 = (bf16[2,256,8,128]{1,3,2,0:T(8,128)(2,1)}, bf16[2,256,8,128]{1,3,2,0:T(8,128)(2,1)S(1)}, u32[]{:S(2)}, u32[]{:S(2)}) collective-permute-start(bf16[2,256,8,128]{1,3,2,0:T(8,128)(2,1)} %get-tuple-element.349), channel_id=1, source_target_pairs={{16,0},{32,16},{48,32},{64,48},{80,64},{96,80},{112,96},{128,112},... | collective-permute-start | bytes 3145736 | tf_op jit(solution)/shard_map/while/body/eval_jaxpr/ppermute | solution.py:24
  420.6 9.6 collective-permute-start
  434.0 23.9 %collective-permute-start.2 = (bf16[2,256,8,128]{1,3,2,0:T(8,128)(2,1)}, bf16[2,256,8,128]{1,3,2,0:T(8,128)(2,1)S(1)}, u32[]{:S(2)}, u32[]{:S(2)}) collective-permute-start(bf16[2,256,8,128]{1,3,2,0:T(8,128)(2,1)} %get-tuple-element.349), channel_id=1, source_target_pairs={{16,0},{32,16},{48,32},{64,48},{80,64},{96,80},{112,96},{128,112},... | collective-permute-start | bytes 3145736 | tf_op jit(solution)/shard_map/while/body/eval_jaxpr/ppermute | solution.py:24
  461.0 10.2 collective-permute-start
  466.3 4.8 collective-permute-start.1
  475.0 23.4 %collective-permute-start.2 = (bf16[2,256,8,128]{1,3,2,0:T(8,128)(2,1)}, bf16[2,256,8,128]{1,3,2,0:T(8,128)(2,1)S(1)}, u32[]{:S(2)}, u32[]{:S(2)}) collective-permute-start(bf16[2,256,8,128]{1,3,2,0:T(8,128)(2,1)} %get-tuple-element.349), channel_id=1, source_target_pairs={{16,0},{32,16},{48,32},{64,48},{80,64},{96,80},{112,96},{128,112},... | collective-permute-start | bytes 3145736 | tf_op jit(solution)/shard_map/while/body/eval_jaxpr/ppermute | solution.py:24
  501.4 10.2 collective-permute-start
  506.8 4.8 collective-permute-start.1
  515.4 23.3 %collective-permute-start.2 = (bf16[2,256,8,128]{1,3,2,0:T(8,128)(2,1)}, bf16[2,256,8,128]{1,3,2,0:T(8,128)(2,1)S(1)}, u32[]{:S(2)}, u32[]{:S(2)}) collective-permute-start(bf16[2,256,8,128]{1,3,2,0:T(8,128)(2,1)} %get-tuple-element.349), channel_id=1, source_target_pairs={{16,0},{32,16},{48,32},{64,48},{80,64},{96,80},{112,96},{128,112},... | collective-permute-start | bytes 3145736 | tf_op jit(solution)/shard_map/while/body/eval_jaxpr/ppermute | solution.py:24
  541.7 10.2 collective-permute-start
  547.1 4.8 collective-permute-start.1
  555.7 23.1 %collective-permute-start.2 = (bf16[2,256,8,128]{1,3,2,0:T(8,128)(2,1)}, bf16[2,256,8,128]{1,3,2,0:T(8,128)(2,1)S(1)}, u32[]{:S(2)}, u32[]{:S(2)}) collective-permute-start(bf16[2,256,8,128]{1,3,2,0:T(8,128)(2,1)} %get-tuple-element.349), channel_id=1, source_target_pairs={{16,0},{32,16},{48,32},{64,48},{80,64},{96,80},{112,96},{128,112},... | collective-permute-start | bytes 3145736 | tf_op jit(solution)/shard_map/while/body/eval_jaxpr/ppermute | solution.py:24
  581.8 10.2 collective-permute-start
  587.1 4.8 collective-permute-start.1
  595.8 272.5 %collective-permute-start.2 = (bf16[2,256,8,128]{1,3,2,0:T(8,128)(2,1)}, bf16[2,256,8,128]{1,3,2,0:T(8,128)(2,1)S(1)}, u32[]{:S(2)}, u32[]{:S(2)}) collective-permute-start(bf16[2,256,8,128]{1,3,2,0:T(8,128)(2,1)} %get-tuple-element.349), channel_id=1, source_target_pairs={{16,0},{32,16},{48,32},{64,48},{80,64},{96,80},{112,96},{128,112},... | collective-permute-start | bytes 3145736 | tf_op jit(solution)/shard_map/while/body/eval_jaxpr/ppermute | solution.py:24
  871.2 10.4 collective-permute-start
  903.8 22.1 %collective-permute-start.2 = (bf16[2,256,8,128]{1,3,2,0:T(8,128)(2,1)}, bf16[2,256,8,128]{1,3,2,0:T(8,128)(2,1)S(1)}, u32[]{:S(2)}, u32[]{:S(2)}) collective-permute-start(bf16[2,256,8,128]{1,3,2,0:T(8,128)(2,1)} %get-tuple-element.349), channel_id=1, source_target_pairs={{16,0},{32,16},{48,32},{64,48},{80,64},{96,80},{112,96},{128,112},... | collective-permute-start | bytes 3145736 | tf_op jit(solution)/shard_map/while/body/eval_jaxpr/ppermute | solution.py:24
  (69 other events, 623.9 us)
Sparse Core Ops, SparseCore 0:
  930.8 213.6 all-gather.2
